TPU v7x, 512 devices: a whole 4x8x8 slice. The times are simulated.
512 devices in a mesh: group: 16 (over x, z_hi), shard: 32 (over y, z_lo, core).
Axes of the slice: x: 4, y: 8, z: 8 (z_hi: 4, z_lo: 2; z = z_hi * 2 + z_lo), core: 2. Of those that a mesh axis runs over, the one named last changes fastest.
Arguments:
- tokens: bfloat16 [32768, 2048], P(('group', 'shard')), may hold values from -7 to 7
- w_qk: bfloat16 [2048, 1024], P('shard'), may hold values from -0.09375 to 0.09375
- w_in: bfloat16 [128, 2048], replicated, may hold values from -0.5 to 0.5
- w_out: bfloat16 [2048, 128], replicated, may hold values from -0.125 to 0.125
- particles: bfloat16 [2097152, 128], P(('group', 'shard')), may hold values from -6 to 6
- cotangent: bfloat16 [2097152, 128], P(('group', 'shard')), may hold values from -6 to 6
- clusters: int32 [2097152], P(('group', 'shard')), may hold values from 0 to 63
- owners: int32 [16384], P(('group', 'shard')), may hold values from 0 to 31, as said below
Outputs:
- particle_out: bfloat16 [2097152, 128], P(('group', 'shard'))
- qk_grad: float32 [2048, 1024], P('shard')
Inputs may be any that keep to these rules, and one draw needn't show every extreme that they name: `owners`: each device's blocks name one owner at most 2 times; in every group some owner is named exactly 2 times by the blocks of every device of the group.
All inputs are finite; a program needn't handle non-finite values.
Results may differ from a plain program's by a relative error of at most 0.028.
Values may be sent and summed in bfloat16 or wider, within the bound.
A program may use at most 64 MiB of HBM per device.

v0:
```python
import math
import jax
import jax.numpy as jnp
from jax import lax
from jax.sharding import PartitionSpec as P

HEADS = 8


def token_pass(tokens, pooled, w_qk, w_in, w_out, pooled_grad):
    hidden_sum = tokens.astype(jnp.float32) + jnp.dot(
        pooled, w_in, preferred_element_type=jnp.float32
    )
    hidden = hidden_sum.astype(jnp.bfloat16)
    queries = jnp.dot(hidden, w_qk, preferred_element_type=jnp.float32).astype(jnp.bfloat16)
    num_rows = hidden.shape[0]
    head_cols = queries.shape[1]
    q_heads = queries.reshape(num_rows, HEADS, -1).astype(jnp.float32)
    score_scale = 1.0 / math.sqrt(q_heads.shape[2])
    scores = jnp.einsum("ihd,jhd->hij", q_heads, q_heads) * score_scale
    self_mask = jnp.eye(num_rows, dtype=bool)
    scores = jnp.where(self_mask[None], -1000000000.0, scores)
    row_max = jnp.max(scores, axis=2, keepdims=True)
    weights_exp = jnp.exp(scores - row_max)
    attn_prob = weights_exp / jnp.sum(weights_exp, axis=2, keepdims=True)
    prob_low = lax.optimization_barrier(attn_prob.astype(jnp.bfloat16)).astype(jnp.float32)
    hidden_wide = hidden.astype(jnp.float32)
    values = hidden_wide[:, :head_cols].reshape(num_rows, HEADS, -1)
    attended = jnp.einsum("hij,jhv->ihv", prob_low, values).reshape(num_rows, head_cols)
    output = jnp.concatenate(
        [hidden_wide[:, :head_cols] + attended, hidden_wide[:, head_cols:]], axis=1
    ).astype(jnp.bfloat16)
    unpooled = jnp.dot(output, w_out, preferred_element_type=jnp.float32).astype(jnp.bfloat16)
    out_grad = jnp.dot(pooled_grad, w_out.T, preferred_element_type=jnp.float32).astype(
        jnp.bfloat16
    )
    grad_heads = out_grad[:, :head_cols].reshape(num_rows, HEADS, -1).astype(jnp.float32)
    prob_grad = jnp.einsum("ihv,jhv->hij", grad_heads, values)
    score_grad = (
        attn_prob
        * (prob_grad - jnp.sum(prob_grad * attn_prob, axis=2, keepdims=True))
        * score_scale
    )
    score_low = lax.optimization_barrier(score_grad.astype(jnp.bfloat16)).astype(jnp.float32)
    q_grad = jnp.einsum("hij,jhd->ihd", score_low, q_heads) + jnp.einsum(
        "hji,jhd->ihd", score_low, q_heads
    )
    q_grad = q_grad.reshape(num_rows, -1).astype(jnp.bfloat16)
    return (unpooled, hidden, q_grad)


def local(tokens, w_qk, w_in, w_out, particles, cotangent, clusters, owners):
    n_shard = lax.axis_size("shard")
    num_blocks = owners.shape[0]
    block_rows = particles.shape[0] // num_blocks
    channels = particles.shape[1]
    capacity = 2 * num_blocks // n_shard
    slot_count = n_shard * capacity
    t_rows = tokens.shape[0]
    owner_hot = (owners[:, None] == jnp.arange(n_shard, dtype=jnp.int32)[None, :]).astype(jnp.int32)
    earlier = jnp.cumsum(owner_hot, axis=0) - owner_hot
    slot_rank = jnp.sum(earlier * owner_hot, axis=1)
    target = owners * capacity + slot_rank
    placing = (target[None, :] == jnp.arange(slot_count, dtype=jnp.int32)[:, None]).astype(
        jnp.bfloat16
    )
    feat_rows = particles.reshape(num_blocks, block_rows * channels)
    grad_rows = cotangent.reshape(num_blocks, block_rows * channels)
    send_feat = jnp.dot(placing, feat_rows, preferred_element_type=jnp.float32).astype(jnp.bfloat16)
    send_grad = jnp.dot(placing, grad_rows, preferred_element_type=jnp.float32).astype(jnp.bfloat16)
    label_rows = (clusters.reshape(num_blocks, block_rows) + 1).astype(jnp.float32)
    send_label = (
        jnp.dot(placing.astype(jnp.float32), label_rows, precision=lax.Precision.HIGHEST) - 1.0
    )
    send_feat = send_feat.reshape(n_shard, capacity, block_rows, channels)
    send_grad = send_grad.reshape(n_shard, capacity, block_rows, channels)
    send_label = send_label.astype(jnp.bfloat16).reshape(n_shard, capacity, block_rows)
    got_feat, got_grad, got_label = (
        lax.all_to_all(send_feat, "shard", split_axis=0, concat_axis=0, tiled=True),
        lax.all_to_all(send_grad, "shard", split_axis=0, concat_axis=0, tiled=True),
        lax.all_to_all(send_label, "shard", split_axis=0, concat_axis=0, tiled=True),
    )
    received = slot_count * block_rows
    labels = got_label.reshape(received).astype(jnp.float32)
    member = (labels[None, :] == jnp.arange(t_rows, dtype=jnp.float32)[:, None]).astype(
        jnp.bfloat16
    )
    counts = jnp.sum(member, axis=1, dtype=jnp.float32)
    pooled_sum = jnp.dot(
        member, got_feat.reshape(received, channels), preferred_element_type=jnp.float32
    )
    pooled = (pooled_sum / jnp.maximum(counts, 1.0)[:, None]).astype(jnp.bfloat16)
    pooled_grad = jnp.dot(
        member, got_grad.reshape(received, channels), preferred_element_type=jnp.float32
    ).astype(jnp.bfloat16)
    full_qk = lax.all_gather(w_qk, "shard", axis=0, tiled=True)
    unpooled, hidden, q_grad = token_pass(tokens, pooled, full_qk, w_in, w_out, pooled_grad)
    slot_values = jnp.einsum(
        "ts,tw->sw", member, unpooled, preferred_element_type=jnp.float32
    ).astype(jnp.bfloat16)
    slot_values = slot_values.reshape(n_shard, capacity, block_rows, channels)
    returned = lax.all_to_all(slot_values, "shard", split_axis=0, concat_axis=0, tiled=True)
    returned_rows = jnp.einsum(
        "sb,sx->bx",
        placing,
        returned.reshape(slot_count, block_rows * channels),
        preferred_element_type=jnp.float32,
    )
    returned_rows = returned_rows.reshape(num_blocks * block_rows, channels)
    particle_out = (particles.astype(jnp.float32) + returned_rows).astype(jnp.bfloat16)
    shard_sum = lax.psum_scatter(
        jnp.einsum("td,tk->dk", hidden, q_grad, preferred_element_type=jnp.float32).astype(
            jnp.bfloat16
        ),
        "shard",
        scatter_dimension=0,
        tiled=True,
    )
    qk_grad = lax.psum(shard_sum, "group").astype(jnp.float32)
    return (particle_out, qk_grad)


def solution(mesh):
    placed = (
        P(("group", "shard"), None),
        P("shard", None),
        P(),
        P(),
        P(("group", "shard"), None),
        P(("group", "shard"), None),
        P(("group", "shard")),
        P(("group", "shard")),
    )
    return jax.shard_map(
        local,
        mesh=mesh,
        in_specs=placed,
        out_specs=(P(("group", "shard"), None), P("shard", None)),
        check_vma=False,
    )
```

profile of v0, /device:TPU:8, one launch (start us, length us, event | category | flops | bytes accessed | tf_op | source)
XLA Modules:
  0.0 491.0 jit_solution(13615514162843825497)
XLA Ops:
  7.2 0.0 copy-start
  7.2 0.8 fusion.64
  8.0 0.1 reduce_window_sum.11
  8.0 0.8 select_reduce_fusion
  8.9 0.7 multiply_add_fusion
  9.5 1.5 fusion.22
  11.0 9.5 %all-to-all-start = ((bf16[32,2,128]{2,1,0:T(2,128)(2,1)}), bf16[32,2,128]{2,1,0:T(2,128)(2,1)S(1)}, u32[]{:S(2)}, u32[]{:S(2)}) async-start(bf16[32,2,128]{2,1,0:T(2,128)(2,1)} %bitcast.1), calls=%async_computation | async-start | bytes 32768 | tf_op jit(solution)/shard_map/all_to_all | solution.py:81
  20.5 1.5 reshape.76
  22.0 0.7 fusion.9
  22.7 1.9 copy.49
  24.6 2.9 all-to-all-done
  27.5 5.4 %all-to-all-start.1 = ((bf16[32,2,128,128]{3,2,1,0:T(8,128)(2,1)}), bf16[32,2,128,128]{3,2,1,0:T(8,128)(2,1)S(1)}, u32[]{:S(2)}, u32[]{:S(2)}) async-start(bf16[32,2,128,128]{3,2,1,0:T(8,128)(2,1)} %bitcast.79), calls=%async_computation.1 | async-start | bytes 4194304 | tf_op jit(solution)/shard_map/all_to_all | solution.py:79
  32.9 0.0 all-gather.2.cloned.1.call-start
  33.0 0.7 all-gather.2.cloned.1.call-update
  33.7 2.3 reshape.85
  36.0 1.9 fusion.10
  37.9 1.9 copy.51
  39.8 53.9 %all-to-all-done.1 = bf16[32,2,128,128]{3,2,1,0:T(8,128)(2,1)S(1)} async-done(((bf16[32,2,128,128]{3,2,1,0:T(8,128)(2,1)}), bf16[32,2,128,128]{3,2,1,0:T(8,128)(2,1)S(1)}, u32[]{:S(2)}, u32[]{:S(2)}) %all-to-all-start.1) | async-done | bytes 2097184 | tf_op jit(solution)/shard_map/all_to_all | solution.py:79
  93.6 0.0 copy-start.1
  93.6 5.6 %all-to-all-start.3 = ((bf16[32,2,128,128]{3,2,1,0:T(8,128)(2,1)}), bf16[32,2,128,128]{3,2,1,0:T(8,128)(2,1)}, u32[]{:S(2)}, u32[]{:S(2)}) async-start(bf16[32,2,128,128]{3,2,1,0:T(8,128)(2,1)} %bitcast.78), calls=%async_computation.3 | async-start | bytes 4194304 | tf_op jit(solution)/shard_map/all_to_all | solution.py:80
  99.3 0.0 reduce-scatter.2.cloned.1.call-start
  99.3 0.3 convert_reduce_fusion
  99.7 0.0 copy-done.1
  99.7 1.6 fusion.2
  101.3 54.6 %all-to-all-done.3 = bf16[32,2,128,128]{3,2,1,0:T(8,128)(2,1)} async-done(((bf16[32,2,128,128]{3,2,1,0:T(8,128)(2,1)}), bf16[32,2,128,128]{3,2,1,0:T(8,128)(2,1)}, u32[]{:S(2)}, u32[]{:S(2)}) %all-to-all-start.3) | async-done | bytes 2097184 | tf_op jit(solution)/shard_map/all_to_all | solution.py:80
  155.9 0.0 copy-done
  155.9 2.3 fusion.25
  158.2 0.2 fusion.42
  158.4 0.0 all-gather.2.cloned.1.call-done
  158.4 3.0 fusion.19
  161.4 0.3 fusion.77
  161.7 0.1 fusion.18
  161.8 0.2 fusion.46
  162.0 0.2 fusion.20
  162.2 3.2 convolution_convert_fusion.3
  165.4 0.0 reduce-scatter.2.cloned.1.call-update
  165.4 0.0 all-reduce.2.cloned.1.call-start
  165.5 0.2 convolution_bitcast_fusion
  165.8 1.3 convolution_convert_fusion.2
  167.1 62.9 %all_to_all.20 = bf16[32,2,128,128]{3,2,1,0:T(8,128)(2,1)S(1)} all-to-all(bf16[32,2,128,128]{3,2,1,0:T(8,128)(2,1)S(1)} %bitcast.80), channel_id=1, replica_groups=mesh['group'=16,'shard'=32] {'shard'}, dimensions={0} | all-to-all | bytes 4194304 | tf_op jit(solution)/shard_map/all_to_all | solution.py:102
  230.0 2.8 fusion.3
  232.8 1.7 reshape.84
  234.6 63.5 %reduce-scatter.2.cloned.1.call-done = bf16[64,1024]{1,0:T(8,128)(2,1)} async-done(((bf16[2048,1024]{1,0:T(8,128)(2,1)}), bf16[64,1024]{1,0:T(8,128)(2,1)}) %reduce-scatter.2.cloned.1.call-update) | async-done | bytes 131088 | tf_op jit(solution)/shard_map/reduce_scatter | solution.py:111
  298.1 0.0 all-reduce.2.cloned.1.call-update
  298.1 2.4 add_convert_fusion
  300.5 182.3 %all-reduce.2.cloned.1.call-done = bf16[64,1024]{1,0:T(8,128)(2,1)} async-done(((bf16[64,1024]{1,0:T(8,128)(2,1)}), bf16[64,1024]{1,0:T(8,128)(2,1)}) %all-reduce.2.cloned.1.call-update) | async-done | bytes 131088 | tf_op jit(solution)/shard_map/psum | solution.py:119
  482.9 1.6 convert_element_type.119
  (6 shorter events, 0.1 us)
Async XLA Ops:
  7.2 148.7 %copy-start = (bf16[2048,128]{1,0:T(8,128)(2,1)S(1)}, bf16[2048,128]{1,0:T(8,128)(2,1)}, u32[]{:S(2)}) copy-start(bf16[2048,128]{1,0:T(8,128)(2,1)} %param.11) | copy-start | bytes 1572868
  11.0 16.5 %all-to-all-start = ((bf16[32,2,128]{2,1,0:T(2,128)(2,1)}), bf16[32,2,128]{2,1,0:T(2,128)(2,1)S(1)}, u32[]{:S(2)}, u32[]{:S(2)}) async-start(bf16[32,2,128]{2,1,0:T(2,128)(2,1)} %bitcast.1), calls=%async_computation | async-start | bytes 32768 | tf_op jit(solution)/shard_map/all_to_all | solution.py:81
  27.5 66.1 %all-to-all-start.1 = ((bf16[32,2,128,128]{3,2,1,0:T(8,128)(2,1)}), bf16[32,2,128,128]{3,2,1,0:T(8,128)(2,1)S(1)}, u32[]{:S(2)}, u32[]{:S(2)}) async-start(bf16[32,2,128,128]{3,2,1,0:T(8,128)(2,1)} %bitcast.79), calls=%async_computation.1 | async-start | bytes 4194304 | tf_op jit(solution)/shard_map/all_to_all | solution.py:79
  32.9 125.5 %all-gather.2.cloned.1.call-start = ((), (), s32[]{:S(2)}) async-start(), calls=%async_computation.5 | async-start | bytes 4325376 | tf_op jit(solution)/shard_map/all_gather | solution.py:96
  93.6 6.0 %copy-start.1 = (bf16[128,2048]{1,0:T(8,128)(2,1)S(1)}, bf16[128,2048]{1,0:T(8,128)(2,1)}, u32[]{:S(2)}) copy-start(bf16[128,2048]{1,0:T(8,128)(2,1)} %param.10) | copy-start | bytes 1572868
  93.6 62.2 %all-to-all-start.3 = ((bf16[32,2,128,128]{3,2,1,0:T(8,128)(2,1)}), bf16[32,2,128,128]{3,2,1,0:T(8,128)(2,1)}, u32[]{:S(2)}, u32[]{:S(2)}) async-start(bf16[32,2,128,128]{3,2,1,0:T(8,128)(2,1)} %bitcast.78), calls=%async_computation.3 | async-start | bytes 4194304 | tf_op jit(solution)/shard_map/all_to_all | solution.py:80
  99.3 198.8 %reduce-scatter.2.cloned.1.call-start = ((), (), s32[]{:S(2)}) async-start(), calls=%async_computation.6 | async-start | bytes 4325376 | tf_op jit(solution)/shard_map/reduce_scatter | solution.py:111
  165.4 317.4 %all-reduce.2.cloned.1.call-start = ((), (), s32[]{:S(2)}) async-start(), calls=%async_computation.7 | async-start | bytes 262144 | tf_op jit(solution)/shard_map/psum | solution.py:119
Sparse Core Ops, SparseCore 0:
  35.9 94.9 all-gather.1
  165.6 132.5 reduce-scatter.1
  301.0 181.8 all-reduce.1
where the time goes:
time: 492 us; the launch traced here: 491 us
  waiting for transfers between devices  358 us (73%)
  blocking collectives  62.9 us (13%)
  starting transfers between devices  20.6 us (4%)
  matrix products  19.4 us (4%)
  between operations  13.9 us (3%)
  local copies, waits for them, and re-layouts  9.43 us (2%)
  other arithmetic  6.86 us (1%)
    psum x1, waiting for transfers between devices, local(): qk_grad = lax.psum(shard_sum, 'group').astype(jnp.float32)  182 us
    reduce_scatter x1, waiting for transfers between devices, local(): lax.psum_scatter(jnp.einsum('td,tk->dk', hidden, q_grad, preferred_elemen...  63.5 us
    all_to_all x1, blocking collectives, local(): lax.all_to_all(slot_values, 'shard', split_axis=0, concat_axis=0, tiled=T...  62.9 us
    all_to_all x1, waiting for transfers between devices, local(): lax.all_to_all(send_grad, 'shard', split_axis=0, concat_axis=0, tiled=True)  54.6 us
    all_to_all x1, waiting for transfers between devices, local(): lax.all_to_all(send_feat, 'shard', split_axis=0, concat_axis=0, tiled=True)  53.9 us
  transfers between devices with their start and end apart: 6, of which 5 were waited for; matrix products, arithmetic and copies ran while one was open for 5% of the time, Pallas kernels for 0%

commit v1 on v0

--- a/solution.py
+++ b/solution.py
@@ -5,6 +5,11 @@
 from jax.sharding import PartitionSpec as P
 
 HEADS = 8
+
+
+def add_all(array, axis):
+    parts = lax.all_gather(array, axis)
+    return jnp.sum(parts, axis=0)
 
 
 def token_pass(tokens, pooled, w_qk, w_in, w_out, pooled_grad):
@@ -116,7 +121,7 @@
         scatter_dimension=0,
         tiled=True,
     )
-    qk_grad = lax.psum(shard_sum, "group").astype(jnp.float32)
+    qk_grad = add_all(shard_sum, "group").astype(jnp.float32)
     return (particle_out, qk_grad)
 
 

time: 492 us -> 386 us (0.78)
  blocking collectives: 62.9 us -> 0 us
  waiting for transfers between devices: 358 us -> 308 us
    psum x1 -> x0, waiting for transfers between devices: 182 us -> none  [local(): qk_grad = lax.psum(shard_sum, 'group').astype(jnp.float32)]
    all_gather x0 -> x1, waiting for transfers between devices: none -> 69 us  [add_all(): parts = lax.all_gather(array, axis)]
    reduce_scatter x1, waiting for transfers between devices: 63.5 us -> 127 us  [local(): lax.psum_scatter(jnp.einsum('td,tk->dk', hidden, q_grad, preferred_elemen...]
    all_to_all x1 -> x0, blocking collectives: 62.9 us -> none  [local(): lax.all_to_all(slot_values, 'shard', split_axis=0, concat_axis=0, tiled=T...]
  transfers between devices with their start and end apart: 6 -> 7, of which waited for: 5 -> 5; matrix products, arithmetic and copies ran while one was open for 5% -> 6% of each run, Pallas kernels for 0% -> 0%
where the time goes in v1:
time: 386 us; the launch traced here: 385 us
  waiting for transfers between devices  308 us (80%)
  starting transfers between devices  25.5 us (7%)
  matrix products  20.7 us (5%)
  between operations  13.9 us (4%)
  local copies, waits for them, and re-layouts  9.41 us (2%)
  other arithmetic  7.93 us (2%)
    reduce_scatter x1, waiting for transfers between devices, local(): lax.psum_scatter(jnp.einsum('td,tk->dk', hidden, q_grad, preferred_elemen...  127 us
    all_gather x1, waiting for transfers between devices, add_all(): parts = lax.all_gather(array, axis)  69 us
    all_to_all x1, waiting for transfers between devices, local(): lax.all_to_all(send_grad, 'shard', split_axis=0, concat_axis=0, tiled=True)  54.6 us
    all_to_all x1, waiting for transfers between devices, local(): lax.all_to_all(send_feat, 'shard', split_axis=0, concat_axis=0, tiled=True)  53.9 us
    all_to_all x1, starting transfers between devices, local(): lax.all_to_all(send_label, 'shard', split_axis=0, concat_axis=0, tiled=True)  9.51 us
  transfers between devices with their start and end apart: 7, of which 5 were waited for; matrix products, arithmetic and copies ran while one was open for 6% of the time, Pallas kernels for 0%

profile of v1, /device:TPU:8, one launch (start us, length us, event | category | flops | bytes accessed | tf_op | source)
XLA Modules:
  0.0 385.5 jit_solution(12822318046470879535)
XLA Ops:
  7.2 0.0 copy-start
  7.2 0.8 fusion.64
  8.0 0.1 reduce_window_sum.11
  8.0 0.8 select_reduce_fusion
  8.9 0.7 multiply_add_fusion
  9.5 1.5 fusion.22
  11.0 9.5 %all-to-all-start = ((bf16[32,2,128]{2,1,0:T(2,128)(2,1)}), bf16[32,2,128]{2,1,0:T(2,128)(2,1)S(1)}, u32[]{:S(2)}, u32[]{:S(2)}) async-start(bf16[32,2,128]{2,1,0:T(2,128)(2,1)} %bitcast.1), calls=%async_computation | async-start | bytes 32768 | tf_op jit(solution)/shard_map/all_to_all | solution.py:86
  20.5 1.5 reshape.76
  22.0 0.7 fusion.9
  22.7 1.9 copy.49
  24.6 2.9 all-to-all-done
  27.5 5.4 %all-to-all-start.1 = ((bf16[32,2,128,128]{3,2,1,0:T(8,128)(2,1)}), bf16[32,2,128,128]{3,2,1,0:T(8,128)(2,1)S(1)}, u32[]{:S(2)}, u32[]{:S(2)}) async-start(bf16[32,2,128,128]{3,2,1,0:T(8,128)(2,1)} %bitcast.81), calls=%async_computation.1 | async-start | bytes 4194304 | tf_op jit(solution)/shard_map/all_to_all | solution.py:84
  32.9 0.0 all-gather.4.cloned.1.call-start
  33.0 0.7 all-gather.4.cloned.1.call-update
  33.7 2.3 reshape.85
  36.0 1.9 fusion.10
  37.9 1.9 copy.51
  39.8 53.9 %all-to-all-done.1 = bf16[32,2,128,128]{3,2,1,0:T(8,128)(2,1)S(1)} async-done(((bf16[32,2,128,128]{3,2,1,0:T(8,128)(2,1)}), bf16[32,2,128,128]{3,2,1,0:T(8,128)(2,1)S(1)}, u32[]{:S(2)}, u32[]{:S(2)}) %all-to-all-start.1) | async-done | bytes 2097184 | tf_op jit(solution)/shard_map/all_to_all | solution.py:84
  93.6 5.6 %all-to-all-start.3 = ((bf16[32,2,128,128]{3,2,1,0:T(8,128)(2,1)}), bf16[32,2,128,128]{3,2,1,0:T(8,128)(2,1)}, u32[]{:S(2)}, u32[]{:S(2)}) async-start(bf16[32,2,128,128]{3,2,1,0:T(8,128)(2,1)} %bitcast.79), calls=%async_computation.3 | async-start | bytes 4194304 | tf_op jit(solution)/shard_map/all_to_all | solution.py:85
  99.3 0.0 reduce-scatter.2.cloned.1.call-start
  99.3 0.3 convert_reduce_fusion
  99.7 0.0 copy-done.1
  99.7 1.6 fusion.2
  101.3 54.6 %all-to-all-done.3 = bf16[32,2,128,128]{3,2,1,0:T(8,128)(2,1)} async-done(((bf16[32,2,128,128]{3,2,1,0:T(8,128)(2,1)}), bf16[32,2,128,128]{3,2,1,0:T(8,128)(2,1)}, u32[]{:S(2)}, u32[]{:S(2)}) %all-to-all-start.3) | async-done | bytes 2097184 | tf_op jit(solution)/shard_map/all_to_all | solution.py:85
  155.9 0.0 copy-done
  155.9 2.3 fusion.25
  158.2 0.2 fusion.42
  158.4 0.0 all-gather.4.cloned.1.call-done
  158.4 3.0 fusion.19
  161.4 0.3 fusion.77
  161.7 0.1 fusion.18
  161.8 0.2 fusion.46
  162.0 0.2 fusion.20
  162.2 3.2 convolution_convert_fusion.3
  165.4 0.0 reduce-scatter.2.cloned.1.call-update
  165.5 0.2 convolution_bitcast_fusion
  165.7 2.6 convolution_convert_fusion.2
  168.4 4.9 %all-to-all-start.2 = ((bf16[32,2,128,128]{3,2,1,0:T(8,128)(2,1)}), bf16[32,2,128,128]{3,2,1,0:T(8,128)(2,1)S(1)}, u32[]{:S(2)}, u32[]{:S(2)}) async-start(bf16[32,2,128,128]{3,2,1,0:T(8,128)(2,1)} %bitcast.82), calls=%async_computation.2 | async-start | bytes 4194304 | tf_op jit(solution)/shard_map/all_to_all | solution.py:107
  173.3 0.0 all-gather.6.cloned.1.call-start
  173.3 127.0 %reduce-scatter.2.cloned.1.call-done = bf16[64,1024]{1,0:T(8,128)(2,1)} async-done(((bf16[2048,1024]{1,0:T(8,128)(2,1)}), bf16[64,1024]{1,0:T(8,128)(2,1)}) %reduce-scatter.2.cloned.1.call-update) | async-done | bytes 131088 | tf_op jit(solution)/shard_map/reduce_scatter | solution.py:116
  300.3 0.0 all-gather.6.cloned.1.call-update
  300.4 0.0 all-to-all-done.2
  300.4 2.8 fusion.3
  303.1 1.7 reshape.84
  304.9 2.4 add_convert_fusion
  307.3 69.0 %all-gather.6.cloned.1.call-done = bf16[1024,1024]{1,0:T(8,128)(2,1)} async-done(((bf16[64,1024]{1,0:T(8,128)(2,1)}), bf16[1024,1024]{1,0:T(8,128)(2,1)}) %all-gather.6.cloned.1.call-update) | async-done | bytes 2097168 | tf_op jit(solution)/shard_map/all_gather | solution.py:11
  376.2 2.0 reduce_sum.52
  378.2 0.7 convert_element_type.121
  (7 shorter events, 0.1 us)
Async XLA Ops:
  7.2 148.7 %copy-start = (bf16[2048,128]{1,0:T(8,128)(2,1)S(1)}, bf16[2048,128]{1,0:T(8,128)(2,1)}, u32[]{:S(2)}) copy-start(bf16[2048,128]{1,0:T(8,128)(2,1)} %param.11) | copy-start | bytes 1572868
  11.0 16.5 %all-to-all-start = ((bf16[32,2,128]{2,1,0:T(2,128)(2,1)}), bf16[32,2,128]{2,1,0:T(2,128)(2,1)S(1)}, u32[]{:S(2)}, u32[]{:S(2)}) async-start(bf16[32,2,128]{2,1,0:T(2,128)(2,1)} %bitcast.1), calls=%async_computation | async-start | bytes 32768 | tf_op jit(solution)/shard_map/all_to_all | solution.py:86
  27.5 66.1 %all-to-all-start.1 = ((bf16[32,2,128,128]{3,2,1,0:T(8,128)(2,1)}), bf16[32,2,128,128]{3,2,1,0:T(8,128)(2,1)S(1)}, u32[]{:S(2)}, u32[]{:S(2)}) async-start(bf16[32,2,128,128]{3,2,1,0:T(8,128)(2,1)} %bitcast.81), calls=%async_computation.1 | async-start | bytes 4194304 | tf_op jit(solution)/shard_map/all_to_all | solution.py:84
  32.9 125.5 %all-gather.4.cloned.1.call-start = ((), (), s32[]{:S(2)}) async-start(), calls=%async_computation.5 | async-start | bytes 4325376 | tf_op jit(solution)/shard_map/all_gather | solution.py:101
  93.6 6.0 %copy-start.1 = (bf16[128,2048]{1,0:T(8,128)(2,1)S(1)}, bf16[128,2048]{1,0:T(8,128)(2,1)}, u32[]{:S(2)}) copy-start(bf16[128,2048]{1,0:T(8,128)(2,1)} %param.10) | copy-start | bytes 1572868
  93.6 62.2 %all-to-all-start.3 = ((bf16[32,2,128,128]{3,2,1,0:T(8,128)(2,1)}), bf16[32,2,128,128]{3,2,1,0:T(8,128)(2,1)}, u32[]{:S(2)}, u32[]{:S(2)}) async-start(bf16[32,2,128,128]{3,2,1,0:T(8,128)(2,1)} %bitcast.79), calls=%async_computation.3 | async-start | bytes 4194304 | tf_op jit(solution)/shard_map/all_to_all | solution.py:85
  99.3 201.1 %reduce-scatter.2.cloned.1.call-start = ((), (), s32[]{:S(2)}) async-start(), calls=%async_computation.6 | async-start | bytes 4325376 | tf_op jit(solution)/shard_map/reduce_scatter | solution.py:116
  168.4 132.0 %all-to-all-start.2 = ((bf16[32,2,128,128]{3,2,1,0:T(8,128)(2,1)}), bf16[32,2,128,128]{3,2,1,0:T(8,128)(2,1)S(1)}, u32[]{:S(2)}, u32[]{:S(2)}) async-start(bf16[32,2,128,128]{3,2,1,0:T(8,128)(2,1)} %bitcast.82), calls=%async_computation.2 | async-start | bytes 4194304 | tf_op jit(solution)/shard_map/all_to_all | solution.py:107
  173.3 202.9 %all-gather.6.cloned.1.call-start = ((), (), s32[]{:S(2)}) async-start(), calls=%async_computation.7 | async-start | bytes 2228224 | tf_op jit(solution)/shard_map/all_gather | solution.py:11
Sparse Core Ops, SparseCore 0:
  35.9 94.9 all-gather.3
  165.5 134.7 reduce-scatter.1
  303.4 72.8 all-gather.5
